TPU v7x, 128 devices: a whole 4x4x4 slice. The times are simulated.
128 devices in a mesh: leaf: 4 (over y_hi, core), front: 32 (over y_lo, z, x).
Axes of the slice: x: 4, y: 4 (y_hi: 2, y_lo: 2; y = y_hi * 2 + y_lo), z: 4, core: 2. Of those that a mesh axis runs over, the one named last changes fastest.
Arguments:
- leaf_source: float32 [4, 2048, 128], P('leaf', 'front'), may hold values from -6 to 6
- mid_source: float32 [4, 2048, 128], P('leaf', 'front'), may hold values from -6 to 6
- root_source: float32 [8192, 128], P('front'), may hold values from -6 to 6
- leaf_inverse: float32 [4, 2, 2048, 2048], P('leaf', None, 'front'), may hold values from -0.09375 to 0.09375
- leaf_coupling: float32 [4, 2, 4096, 2048], P('leaf', None, None, 'front'), may hold values from -0.09375 to 0.09375
- mid_inverse: float32 [4, 2, 2048, 4096], P('leaf', None, None, 'front'), may hold values from -0.0625 to 0.0625
- mid_coupling: float32 [4, 2, 8192, 2048], P('leaf', None, None, 'front'), may hold values from -0.0625 to 0.0625
- root_inverse: float32 [2, 8192, 8192], P(None, 'leaf', 'front'), may hold values from -0.046875 to 0.046875
- leaf_blocks: int32 [4, 32], P('leaf'), may hold values from 0 to 31, as said below
- mid_blocks: int32 [2, 64], replicated, may hold values from 0 to 63, as said below
Outputs:
- leaf_solution: float32 [4, 2048, 128], P('leaf', 'front')
- mid_solution: float32 [4, 2048, 128], P('leaf', 'front')
- root_solution: float32 [8192, 128], P('front')
Inputs may be any that keep to these rules, and one draw needn't show every extreme that they name: `leaf_blocks`: each row holds every block number of a level-1 separator exactly once. `mid_blocks`: each row holds every block number of the root separator exactly once.
All inputs are finite; a program needn't handle non-finite values.
Results may differ from a plain program's by a relative error of at most 0.00015.
Values sent between devices are 32-bit elements; how exact they have to be, the bound alone decides.
A program may use at most 128 MiB of HBM per device.

v0:
```python
import jax
import jax.numpy as jnp
from jax import lax
from jax.sharding import PartitionSpec as P

exact_precision = lax.Precision.HIGHEST


def partner(value, axis, apart):
    return lax.ppermute(value, axis, [(i, i ^ 1 << apart) for i in range(lax.axis_size(axis))])


def complex_apply(matrix, vectors):
    width = vectors.shape[1] // 2
    real_part = jnp.dot(
        matrix[0], vectors, precision=exact_precision, preferred_element_type=jnp.float32
    )
    imag_part = jnp.dot(
        matrix[1], vectors, precision=exact_precision, preferred_element_type=jnp.float32
    )
    return jnp.concatenate(
        [real_part[:, :width] - imag_part[:, width:], real_part[:, width:] + imag_part[:, :width]],
        axis=1,
    )


def complex_transposed(matrix, vectors):
    width = vectors.shape[1] // 2
    dims = (((0,), (0,)), ((), ()))
    real_part = lax.dot_general(
        matrix[0], vectors, dims, precision=exact_precision, preferred_element_type=jnp.float32
    )
    imag_part = lax.dot_general(
        matrix[1], vectors, dims, precision=exact_precision, preferred_element_type=jnp.float32
    )
    return jnp.concatenate(
        [real_part[:, :width] - imag_part[:, width:], real_part[:, width:] + imag_part[:, :width]],
        axis=1,
    )


def pick_rows(matrix, block_order, row_count):
    positions = jnp.arange(row_count, dtype=jnp.int32)
    sources = jnp.take(block_order, positions // 128) * 128 + positions % 128
    return jnp.take(matrix, sources, axis=1)


def gather_rows(local_rows, update, initial):
    return update(initial, lax.all_gather(local_rows, "front", axis=0, tiled=True), jnp.int32(0))


def scatter_rows(term, rows_each):
    return lax.psum_scatter(
        term(jnp.int32(0), rows_each * lax.axis_size("front")),
        "front",
        scatter_dimension=0,
        tiled=True,
    )


def pair_swap(values):
    return partner(values, "leaf", 0)


def group_total(values):
    return lax.psum(values, "leaf")


def body(
    leaf_source,
    mid_source,
    root_source,
    leaf_inverse,
    leaf_coupling,
    mid_inverse,
    mid_coupling,
    root_inverse,
    leaf_blocks,
    mid_blocks,
):
    front_count = lax.axis_size("front")
    group = lax.axis_index("leaf")
    side = group % 2
    source_two = leaf_source[0]
    inverse_two = leaf_inverse[0]
    coupling_two = leaf_coupling[0]
    inverse_one = mid_inverse[0]
    coupling_one = mid_coupling[0]
    order_two = jnp.argsort(leaf_blocks[0])
    order_one = jnp.argsort(lax.dynamic_index_in_dim(mid_blocks, group // 2, 0, keepdims=False))
    width2 = source_two.shape[1]
    rows_two = source_two.shape[0]
    half_rows = mid_source.shape[1]
    block_rows = coupling_two.shape[1] // front_count
    root_block = root_source.shape[0]

    def fold_inverse_two(carry, shard_piece, row_start):
        return complex_apply(inverse_two, shard_piece)

    solved_two = gather_rows(source_two, fold_inverse_two, jnp.zeros(source_two.shape, jnp.float32))

    def lift_two(row_start, row_count):
        return complex_apply(pick_rows(coupling_two, order_two, row_count), solved_two)

    lifted = scatter_rows(lift_two, block_rows)
    placed = lax.dynamic_update_slice_in_dim(
        jnp.zeros((block_rows, width2), jnp.float32), mid_source[0], side * half_rows, 0
    )
    own_part = placed - lifted
    reduced_one = own_part + pair_swap(own_part)

    def apply_one(row_start, row_count):
        return complex_apply(inverse_one, reduced_one)

    solved_one = scatter_rows(apply_one, half_rows)

    def lift_one(row_start, row_count):
        return complex_apply(pick_rows(coupling_one, order_one, row_count), solved_one)

    gathered_terms = group_total(scatter_rows(lift_one, root_block))
    reduced_root = root_source - gathered_terms

    def apply_root(row_start, row_count):
        return complex_apply(root_inverse, reduced_root)

    solved_root = scatter_rows(apply_root, root_inverse.shape[1] // front_count)

    def fold_root(carry, shard_piece, row_start):
        return complex_transposed(root_inverse, shard_piece)

    partial_root = gather_rows(solved_root, fold_root, jnp.zeros(root_source.shape, jnp.float32))
    root_solution = group_total(partial_root)

    def fold_mid(carry, shard_piece, row_start):
        return complex_transposed(
            pick_rows(coupling_one, order_one, shard_piece.shape[0]), shard_piece
        )

    pulled_one = gather_rows(root_solution, fold_mid, jnp.zeros(solved_one.shape, jnp.float32))
    rest_one = solved_one - pulled_one

    def fold_inverse_one(carry, shard_piece, row_start):
        return complex_transposed(inverse_one, shard_piece)

    own_columns = gather_rows(
        rest_one, fold_inverse_one, jnp.zeros((block_rows, width2), jnp.float32)
    )
    mid_block = own_columns + pair_swap(own_columns)
    mid_solution = lax.dynamic_slice_in_dim(mid_block, side * half_rows, half_rows, 0)

    def fold_leaf(carry, shard_piece, row_start):
        return complex_transposed(
            pick_rows(coupling_two, order_two, shard_piece.shape[0]), shard_piece
        )

    pulled_two = gather_rows(mid_block, fold_leaf, jnp.zeros(solved_two.shape, jnp.float32))
    rest_two = solved_two - pulled_two

    def apply_leaf_back(row_start, row_count):
        return complex_transposed(inverse_two, rest_two)

    leaf_solution = scatter_rows(apply_leaf_back, rows_two)
    return (leaf_solution[None], mid_solution[None], root_solution)


def solution(mesh):
    placed = (
        P("leaf", "front", None),
        P("leaf", "front", None),
        P("front", None),
        P("leaf", None, "front", None),
        P("leaf", None, None, "front"),
        P("leaf", None, None, "front"),
        P("leaf", None, None, "front"),
        P(None, "leaf", "front"),
        P("leaf", None),
        P(),
    )
    return jax.shard_map(
        body,
        mesh=mesh,
        in_specs=placed,
        out_specs=(P("leaf", "front", None), P("leaf", "front", None), P("front", None)),
        check_vma=False,
    )
```

profile of v0, /device:TPU:0, one launch (start us, length us, event | category | flops | bytes accessed | tf_op | source)
XLA Modules:
  0.0 1807.4 jit_solution(7411422771738973150)
XLA Ops:
  11.7 6.2 copy.32
  17.8 19.9 %broadcast_clamp_fusion.1 = s32[4096]{0:T(1024)S(1)} fusion(s32[]{:T(128)} %bitcast.35, s32[]{:T(128)} %bitcast.34, s32[]{:T(128)} %bitcast.33, s32[]{:T(128)} %bitcast.32, s32[]{:T(128)} %bitcast.31, s32[]{:T(128)} %bitcast.30, s32[]{:T(128)} %bitcast.29, s32[]{:T(128)} %bitcast.28, s32[]{:T(128)} %bitcast.27, s32[]{:T(128)} %bitcast.26, s32[]{:T(128)} %bitcast.25, ...), kind=kLoop, calls=%fused_computation.211 | loop fusion | flops 356352 | bytes 16512 | tf_op gather
  37.7 30.5 %gather_fusion = f32[4096,2,64]{2,1,0:T(2,128)} fusion(f32[2,4096,64]{2,0,1:T(2,128)} %bitcast.203, s32[4096]{0:T(1024)S(1)} %broadcast_clamp_fusion.1), kind=kCustom, calls=%fused_computation.clone | custom fusion | bytes 4210688 | tf_op jit(solution)/shard_map/jit(_take)/gather | solution.py:45
  68.3 19.9 %compare_and_fusion.1 = pred[4096]{0:T(1024)(128)(4,1)S(1)} fusion(s32[]{:T(128)} %bitcast.35, s32[]{:T(128)} %bitcast.34, s32[]{:T(128)} %bitcast.33, s32[]{:T(128)} %bitcast.32, s32[]{:T(128)} %bitcast.31, s32[]{:T(128)} %bitcast.30, s32[]{:T(128)} %bitcast.29, s32[]{:T(128)} %bitcast.28, s32[]{:T(128)} %bitcast.27, s32[]{:T(128)} %bitcast.26, ...), kind=kLoop, calls=%fused_computation.210 | loop fusion | flops 364544 | bytes 4224 | tf_op jit(solution)/shard_map/jit(_take)/and | solution.py:45
  88.2 16.3 select_bitcast_fusion.1
  108.6 54.6 %all-gather.15.cloned.1.call-done = f32[1,2048,128]{2,1,0:T(8,128)} async-done(((f32[1,64,128]{2,1,0:T(8,128)}), f32[1,2048,128]{2,1,0:T(8,128)}) %all-gather.15.cloned.1.call-update) | async-done | bytes 1048592 | tf_op jit(solution)/shard_map/all_gather | solution.py:49
  179.1 39.6 %compare_and_fusion = (pred[8192]{0:T(1024)(128)(4,1)S(1)}, s32[8192]{0:T(1024)S(1)}) fusion(s32[]{:T(128)} %bitcast.109, s32[]{:T(128)} %bitcast.108, s32[]{:T(128)} %bitcast.107, s32[]{:T(128)} %bitcast.106, s32[]{:T(128)} %bitcast.105, s32[]{:T(128)} %bitcast.104, s32[]{:T(128)} %bitcast.103, s32[]{:T(128)} %bitcast.102, s32[]{:T(128)} %bitcast.101, ...), kind=kLoop, calls=%fused_computation.166 | loop fusion | flops 1253376 | bytes 41216 | tf_op jit(solution)/shard_map/jit(_take)/and | solution.py:45
  218.7 118.7 %reduce-scatter.12.cloned.1.call-done = f32[128,128]{0,1:T(8,128)} async-done(((f32[4096,128]{0,1:T(8,128)}), f32[128,128]{0,1:T(8,128)}) %reduce-scatter.12.cloned.1.call-update) | async-done | bytes 65552 | tf_op jit(solution)/shard_map/reduce_scatter | solution.py:53
  338.5 10.8 copy.34
  349.3 59.6 %gather_fusion.1 = f32[8192,2,64]{2,1,0:T(2,128)} fusion(f32[2,8192,64]{2,0,1:T(2,128)} %bitcast.198, s32[8192]{0:T(1024)S(1)} %broadcast_clamp_fusion), kind=kCustom, calls=%fused_computation.1.clone | custom fusion | bytes 8421376 | tf_op jit(solution)/shard_map/jit(_take)/gather | solution.py:45
  417.3 29.5 %select_bitcast_fusion = f32[2,8192,64]{2,0,1:T(2,128)S(1)} fusion(f32[8192,2,64]{2,1,0:T(2,128)} %gather_fusion.1, pred[8192]{0:T(1024)(128)(4,1)S(1)} %get-tuple-element.20), kind=kLoop, calls=%fused_computation.2 | loop fusion | flops 1048576 | bytes 8396800 | tf_op jit(solution)/shard_map/jit(_take)/select_n | solution.py:45
  446.8 7.7 fusion.157
  454.5 120.2 %reduce-scatter.16.cloned.1.call-done = f32[64,128]{1,0:T(8,128)} async-done(((f32[2048,128]{1,0:T(8,128)}), f32[64,128]{1,0:T(8,128)}) %reduce-scatter.16.cloned.1.call-update) | async-done | bytes 32784
  588.1 165.2 %reduce-scatter.14.cloned.1.call-done = f32[256,128]{0,1:T(8,128)} async-done(((f32[8192,128]{0,1:T(8,128)}), f32[256,128]{0,1:T(8,128)}) %reduce-scatter.14.cloned.1.call-update) | async-done | bytes 131088 | tf_op jit(solution)/shard_map/reduce_scatter | solution.py:53
  753.9 38.4 %all-reduce.3.cloned.1.call-done = f32[256,128]{0,1:T(8,128)} async-done(((f32[256,128]{0,1:T(8,128)}), f32[256,128]{0,1:T(8,128)}) %all-reduce.3.cloned.1.call-update) | async-done | bytes 131088 | tf_op jit(solution)/shard_map/psum | solution.py:66
  803.9 160.8 %reduce-scatter.18.cloned.1.call-done = f32[64,128]{1,0:T(8,128)} async-done(((f32[2048,128]{1,0:T(8,128)}), f32[64,128]{1,0:T(8,128)}) %reduce-scatter.18.cloned.1.call-update) | async-done | bytes 32784 | tf_op jit(solution)/shard_map/reduce_scatter | solution.py:53
  964.8 148.6 %all-gather.7.cloned.1.call-done = f32[2048,128]{1,0:T(8,128)} async-done(((f32[64,128]{1,0:T(8,128)}), f32[2048,128]{1,0:T(8,128)}) %all-gather.7.cloned.1.call-update) | async-done | bytes 1048592 | tf_op jit(solution)/shard_map/all_gather | solution.py:49
  1121.7 40.5 %all-reduce.5.cloned.1.call-done = f32[256,128]{0,1:T(8,128)} async-done(((f32[256,128]{0,1:T(8,128)}), f32[256,128]{0,1:T(8,128)}) %all-reduce.5.cloned.1.call-update) | async-done | bytes 131088 | tf_op jit(solution)/shard_map/psum | solution.py:66
  1162.4 158.7 %all-gather.9.cloned.1.call-done = f32[8192,128]{0,1:T(8,128)} async-done(((f32[256,128]{0,1:T(8,128)}), f32[8192,128]{0,1:T(8,128)}) %all-gather.9.cloned.1.call-update) | async-done | bytes 4194320 | tf_op jit(solution)/shard_map/all_gather | solution.py:49
  1321.1 10.3 fusion.169
  1331.5 7.1 fusion.170
  1339.4 150.8 %all-gather.11.cloned.1.call-done = f32[2048,128]{1,0:T(8,128)} async-done(((f32[64,128]{1,0:T(8,128)}), f32[2048,128]{1,0:T(8,128)}) %all-gather.11.cloned.1.call-update) | async-done | bytes 1048592 | tf_op jit(solution)/shard_map/all_gather | solution.py:49
  1499.0 125.6 %all-gather.13.cloned.1.call-done = f32[4096,128]{0,1:T(8,128)} async-done(((f32[128,128]{0,1:T(8,128)}), f32[4096,128]{0,1:T(8,128)}) %all-gather.13.cloned.1.call-update) | async-done | bytes 2097168 | tf_op jit(solution)/shard_map/all_gather | solution.py:49
  1639.5 159.1 %reduce-scatter.20.cloned.1.call-done = f32[64,128]{1,0:T(8,128)} async-done(((f32[2048,128]{1,0:T(8,128)}), f32[64,128]{1,0:T(8,128)}) %reduce-scatter.20.cloned.1.call-update) | async-done | bytes 32784
  (118 shorter events, 93.6 us)
Async XLA Ops:
  7.2 166.6 %copy-start = (s32[2,64]{1,0:T(2,128)S(1)}, s32[2,64]{1,0:T(2,128)}, u32[]{:S(2)}) copy-start(s32[2,64]{1,0:T(2,128)} %param.27) | copy-start | bytes 1540
  7.2 156.1 %all-gather.15.cloned.1.call-start = ((), (), s32[]{:S(2)}) async-start(), calls=%async_computation.13 | async-start | bytes 1081344 | tf_op jit(solution)/shard_map/all_gather | solution.py:49
  7.9 329.5 %reduce-scatter.12.cloned.1.call-start = ((), (), s32[]{:S(2)}) async-start(), calls=%async_computation.5 | async-start | bytes 2162688 | tf_op jit(solution)/shard_map/reduce_scatter | solution.py:53
  104.5 58.7 %copy-start.7 = (f32[1,2,64,2048]{3,2,1,0:T(8,128)S(1)}, f32[1,2,64,2048]{3,2,1,0:T(8,128)}, u32[]{:S(2)}) copy-start(f32[1,2,64,2048]{3,2,1,0:T(8,128)} %param.21) | copy-start | bytes 3145732
  163.2 4.3 copy-start.4
  173.6 401.1 %reduce-scatter.16.cloned.1.call-start = ((), (), s32[]{:S(2)}) async-start(), calls=%async_computation.14 | async-start | bytes 1081344
  338.3 70.6 %collective-permute-start = (f32[128,128]{0,1:T(8,128)S(1)}, f32[128,128]{0,1:T(8,128)S(1)}, u32[]{:S(2)}, u32[]{:S(2)}) collective-permute-start(f32[128,128]{0,1:T(8,128)S(1)} %sub.65), channel_id=1, source_target_pairs={{0,32},{32,0},{64,96},{96,64},{1,33},{33,1},{65,97},{97,65},{2,34}... | collective-permute-start | bytes 196616 | tf_op jit(solution)/shard_map/ppermute | solution.py:10
  417.2 336.1 %reduce-scatter.14.cloned.1.call-start = ((), (), s32[]{:S(2)}) async-start(), calls=%async_computation.6 | async-start | bytes 4325376 | tf_op jit(solution)/shard_map/reduce_scatter | solution.py:53
  574.7 6.1 copy-start.2
  574.7 6.1 copy-start.10
  588.0 165.7 %copy-start.11 = (f32[256,128]{1,0:T(8,128)S(1)}, f32[256,128]{1,0:T(8,128)}, u32[]{:S(2)}) copy-start(f32[256,128]{1,0:T(8,128)} %param.20) | copy-start | bytes 393220
  588.0 204.2 %all-reduce.3.cloned.1.call-start = ((), (), s32[]{:S(2)}) async-start(), calls=%async_computation.7 | async-start | bytes 262144 | tf_op jit(solution)/shard_map/psum | solution.py:66
  753.3 211.5 %reduce-scatter.18.cloned.1.call-start = ((), (), s32[]{:S(2)}) async-start(), calls=%async_computation.15 | async-start | bytes 1081344 | tf_op jit(solution)/shard_map/reduce_scatter | solution.py:53
  803.9 309.5 %all-gather.7.cloned.1.call-start = ((), (), s32[]{:S(2)}) async-start(), calls=%async_computation.8 | async-start | bytes 1081344 | tf_op jit(solution)/shard_map/all_gather | solution.py:49
  964.8 197.4 %all-reduce.5.cloned.1.call-start = ((), (), s32[]{:S(2)}) async-start(), calls=%async_computation.9 | async-start | bytes 262144 | tf_op jit(solution)/shard_map/psum | solution.py:66
  1121.7 199.5 %all-gather.9.cloned.1.call-start = ((), (), s32[]{:S(2)}) async-start(), calls=%async_computation.10 | async-start | bytes 4325376 | tf_op jit(solution)/shard_map/all_gather | solution.py:49
  1162.2 328.1 %all-gather.11.cloned.1.call-start = ((), (), s32[]{:S(2)}) async-start(), calls=%async_computation.11 | async-start | bytes 1081344 | tf_op jit(solution)/shard_map/all_gather | solution.py:49
  1321.1 10.3 copy-start.3
  1321.1 10.4 copy-start.5
  1339.4 285.2 %all-gather.13.cloned.1.call-start = ((), (), s32[]{:S(2)}) async-start(), calls=%async_computation.12 | async-start | bytes 2162688 | tf_op jit(solution)/shard_map/all_gather | solution.py:49
  1497.0 1.3 collective-permute-start.1
  1499.0 299.6 %reduce-scatter.20.cloned.1.call-start = ((), (), s32[]{:S(2)}) async-start(), calls=%async_computation.16 | async-start | bytes 1081344
  1624.6 5.8 copy-start.6
  1635.2 165.0 %copy-start.1 = (s32[2,64]{1,0:T(2,128)S(1)}, s32[2,64]{1,0:T(2,128)}, u32[]{:S(2)}) copy-start(s32[2,64]{1,0:T(2,128)} %param.27) | copy-start | bytes 1540
  (3 other events, 5.6 us)
Sparse Core Ops, SparseCore 0:
  9.7 153.5 all-gather.14
  173.7 163.6 reduce-scatter.11
  417.3 157.3 reduce-scatter.15
  588.2 165.0 reduce-scatter.13
  755.6 36.6 all-reduce.2
  804.0 160.7 reduce-scatter.17
  966.4 146.9 all-gather.6
  1121.8 40.3 all-reduce.4
  1163.9 157.1 all-gather.8
  1339.5 150.7 all-gather.10
  1499.1 125.4 all-gather.12
  1638.0 160.5 reduce-scatter.19
where the time goes:
time: 1820 us; the launch traced here: 1810 us
  waiting for transfers between devices  1440 us (79%)
  other arithmetic  140 us (8%)
  local copies, waits for them, and re-layouts  133 us (7%)
  matrix products  74.3 us (4%)
    all_gather x5, waiting for transfers between devices, gather_rows(): lax.all_gather(local_rows, 'front', axis=0, tiled=True)  638 us
    reduce_scatter x3, waiting for transfers between devices, scatter_rows(): lax.psum_scatter(term(jnp.int32(0), rows_each * lax.axis_size('front')),...  445 us
    unnamed x14, waiting for transfers between devices  280 us
    gather x2, local copies, waits for them, and re-layouts, pick_rows(): return jnp.take(matrix, sources, axis=1)  90.1 us
    psum x2, waiting for transfers between devices, group_total(): return lax.psum(values, 'leaf')  78.9 us
    and x2, other arithmetic, pick_rows(): return jnp.take(matrix, sources, axis=1)  59.5 us
    select_n x2, other arithmetic, pick_rows(): return jnp.take(matrix, sources, axis=1)  45.9 us
  transfers between devices with their start and end apart: 14, of which 13 were waited for; matrix products, arithmetic and copies ran while one was open for 14% of the time, Pallas kernels for 0%

commit v1 on v0

--- a/solution.py
+++ b/solution.py
@@ -63,7 +63,7 @@
 
 
 def group_total(values):
-    return lax.psum(values, "leaf")
+    return jnp.sum(lax.all_gather(values, "leaf"), axis=0)
 
 
 def body(

time: 1820 us -> 1760 us (0.967)
  waiting for transfers between devices: 1440 us -> 1360 us
  blocking collectives: 0 us -> 18.8 us
    psum x2 -> x0, waiting for transfers between devices: 78.9 us -> none  [group_total(): return lax.psum(values, 'leaf')]
    all_gather x0 -> x2, blocking collectives: none -> 18.8 us  [group_total(): return jnp.sum(lax.all_gather(values, 'leaf'), axis=0)]
    unnamed x14 -> x12, waiting for transfers between devices: 280 us -> 281 us
  transfers between devices with their start and end apart: 14 -> 12, of which waited for: 13 -> 11; matrix products, arithmetic and copies ran while one was open for 14% -> 15% of each run, Pallas kernels for 0% -> 0%
where the time goes in v1:
time: 1760 us; the launch traced here: 1750 us
  waiting for transfers between devices  1360 us (77%)
  other arithmetic  143 us (8%)
  local copies, waits for them, and re-layouts  139 us (8%)
  matrix products  74.1 us (4%)
  blocking collectives  18.8 us (1%)
    all_gather x5, waiting for transfers between devices, gather_rows(): lax.all_gather(local_rows, 'front', axis=0, tiled=True)  638 us
    reduce_scatter x3, waiting for transfers between devices, scatter_rows(): lax.psum_scatter(term(jnp.int32(0), rows_each * lax.axis_size('front')),...  439 us
    unnamed x12, waiting for transfers between devices  281 us
    gather x2, local copies, waits for them, and re-layouts, pick_rows(): return jnp.take(matrix, sources, axis=1)  90.1 us
    and x2, other arithmetic, pick_rows(): return jnp.take(matrix, sources, axis=1)  59.7 us
    select_n x2, other arithmetic, pick_rows(): return jnp.take(matrix, sources, axis=1)  45.9 us
  transfers between devices with their start and end apart: 12, of which 11 were waited for; matrix products, arithmetic and copies ran while one was open for 15% of the time, Pallas kernels for 0%

profile of v1, /device:TPU:0, one launch (start us, length us, event | category | flops | bytes accessed | tf_op | source)
XLA Modules:
  0.0 1748.6 jit_solution(16314909267873274272)
XLA Ops:
  11.7 6.2 copy.28
  17.9 19.9 %broadcast_clamp_fusion.1 = s32[4096]{0:T(1024)S(1)} fusion(s32[]{:T(128)} %bitcast.35, s32[]{:T(128)} %bitcast.34, s32[]{:T(128)} %bitcast.33, s32[]{:T(128)} %bitcast.32, s32[]{:T(128)} %bitcast.31, s32[]{:T(128)} %bitcast.30, s32[]{:T(128)} %bitcast.29, s32[]{:T(128)} %bitcast.28, s32[]{:T(128)} %bitcast.27, s32[]{:T(128)} %bitcast.26, s32[]{:T(128)} %bitcast.25, ...), kind=kLoop, calls=%fused_computation.211 | loop fusion | flops 356352 | bytes 16512 | tf_op gather
  37.8 30.5 %gather_fusion = f32[4096,2,64]{2,1,0:T(2,128)} fusion(f32[2,4096,64]{2,0,1:T(2,128)} %bitcast.207, s32[4096]{0:T(1024)S(1)} %broadcast_clamp_fusion.1), kind=kCustom, calls=%fused_computation.clone | custom fusion | bytes 4210688 | tf_op jit(solution)/shard_map/jit(_take)/gather | solution.py:45
  68.4 20.0 %compare_and_fusion.1 = pred[4096]{0:T(1024)(128)(4,1)S(1)} fusion(s32[]{:T(128)} %bitcast.35, s32[]{:T(128)} %bitcast.34, s32[]{:T(128)} %bitcast.33, s32[]{:T(128)} %bitcast.32, s32[]{:T(128)} %bitcast.31, s32[]{:T(128)} %bitcast.30, s32[]{:T(128)} %bitcast.29, s32[]{:T(128)} %bitcast.28, s32[]{:T(128)} %bitcast.27, s32[]{:T(128)} %bitcast.26, ...), kind=kLoop, calls=%fused_computation.210 | loop fusion | flops 364544 | bytes 4224 | tf_op jit(solution)/shard_map/jit(_take)/and | solution.py:45
  88.3 16.3 select_bitcast_fusion.1
  108.8 54.6 %all-gather.17.cloned.1.call-done = f32[1,2048,128]{2,1,0:T(8,128)} async-done(((f32[1,64,128]{2,1,0:T(8,128)}), f32[1,2048,128]{2,1,0:T(8,128)}) %all-gather.17.cloned.1.call-update) | async-done | bytes 1048592 | tf_op jit(solution)/shard_map/all_gather | solution.py:49
  179.2 39.7 %compare_and_fusion = (pred[8192]{0:T(1024)(128)(4,1)S(1)}, s32[8192]{0:T(1024)S(1)}) fusion(s32[]{:T(128)} %bitcast.109, s32[]{:T(128)} %bitcast.108, s32[]{:T(128)} %bitcast.107, s32[]{:T(128)} %bitcast.106, s32[]{:T(128)} %bitcast.105, s32[]{:T(128)} %bitcast.104, s32[]{:T(128)} %bitcast.103, s32[]{:T(128)} %bitcast.102, s32[]{:T(128)} %bitcast.101, ...), kind=kLoop, calls=%fused_computation.166 | loop fusion | flops 1253376 | bytes 41216 | tf_op jit(solution)/shard_map/jit(_take)/and | solution.py:45
  218.9 118.5 %reduce-scatter.12.cloned.1.call-done = f32[128,128]{0,1:T(8,128)} async-done(((f32[4096,128]{0,1:T(8,128)}), f32[128,128]{0,1:T(8,128)}) %reduce-scatter.12.cloned.1.call-update) | async-done | bytes 65552 | tf_op jit(solution)/shard_map/reduce_scatter | solution.py:53
  338.4 10.8 copy.30
  349.2 59.5 %gather_fusion.1 = f32[8192,2,64]{2,1,0:T(2,128)} fusion(f32[2,8192,64]{2,0,1:T(2,128)} %bitcast.202, s32[8192]{0:T(1024)S(1)} %broadcast_clamp_fusion), kind=kCustom, calls=%fused_computation.1.clone | custom fusion | bytes 8421376 | tf_op jit(solution)/shard_map/jit(_take)/gather | solution.py:45
  417.2 29.5 %select_bitcast_fusion = f32[2,8192,64]{2,0,1:T(2,128)S(1)} fusion(f32[8192,2,64]{2,1,0:T(2,128)} %gather_fusion.1, pred[8192]{0:T(1024)(128)(4,1)S(1)} %get-tuple-element.20), kind=kLoop, calls=%fused_computation.2 | loop fusion | flops 1048576 | bytes 8396800 | tf_op jit(solution)/shard_map/jit(_take)/select_n | solution.py:45
  446.7 7.7 fusion.157
  454.5 120.6 %reduce-scatter.16.cloned.1.call-done = f32[64,128]{1,0:T(8,128)} async-done(((f32[2048,128]{1,0:T(8,128)}), f32[64,128]{1,0:T(8,128)}) %reduce-scatter.16.cloned.1.call-update) | async-done | bytes 32784
  589.3 163.8 %reduce-scatter.14.cloned.1.call-done = f32[256,128]{0,1:T(8,128)} async-done(((f32[8192,128]{0,1:T(8,128)}), f32[256,128]{0,1:T(8,128)}) %reduce-scatter.14.cloned.1.call-update) | async-done | bytes 131088 | tf_op jit(solution)/shard_map/reduce_scatter | solution.py:53
  753.1 9.9 all-gather.1
  778.0 156.6 %reduce-scatter.18.cloned.1.call-done = f32[64,128]{1,0:T(8,128)} async-done(((f32[2048,128]{1,0:T(8,128)}), f32[64,128]{1,0:T(8,128)}) %reduce-scatter.18.cloned.1.call-update) | async-done | bytes 32784 | tf_op jit(solution)/shard_map/reduce_scatter | solution.py:53
  934.6 149.3 %all-gather.9.cloned.1.call-done = f32[2048,128]{1,0:T(8,128)} async-done(((f32[64,128]{1,0:T(8,128)}), f32[2048,128]{1,0:T(8,128)}) %all-gather.9.cloned.1.call-update) | async-done | bytes 1048592 | tf_op jit(solution)/shard_map/all_gather | solution.py:49
  1091.5 8.8 all-gather.2
  1104.7 157.6 %all-gather.11.cloned.1.call-done = f32[8192,128]{0,1:T(8,128)} async-done(((f32[256,128]{0,1:T(8,128)}), f32[8192,128]{0,1:T(8,128)}) %all-gather.11.cloned.1.call-update) | async-done | bytes 4194320 | tf_op jit(solution)/shard_map/all_gather | solution.py:49
  1262.3 10.3 fusion.169
  1272.6 7.1 fusion.170
  1280.6 150.8 %all-gather.13.cloned.1.call-done = f32[2048,128]{1,0:T(8,128)} async-done(((f32[64,128]{1,0:T(8,128)}), f32[2048,128]{1,0:T(8,128)}) %all-gather.13.cloned.1.call-update) | async-done | bytes 1048592 | tf_op jit(solution)/shard_map/all_gather | solution.py:49
  1440.2 125.6 %all-gather.15.cloned.1.call-done = f32[4096,128]{0,1:T(8,128)} async-done(((f32[128,128]{0,1:T(8,128)}), f32[4096,128]{0,1:T(8,128)}) %all-gather.15.cloned.1.call-update) | async-done | bytes 2097168 | tf_op jit(solution)/shard_map/all_gather | solution.py:49
  1580.7 159.2 %reduce-scatter.20.cloned.1.call-done = f32[64,128]{1,0:T(8,128)} async-done(((f32[2048,128]{1,0:T(8,128)}), f32[64,128]{1,0:T(8,128)}) %reduce-scatter.20.cloned.1.call-update) | async-done | bytes 32784
  (118 shorter events, 100.7 us)
Async XLA Ops:
  7.2 166.7 %copy-start = (s32[2,64]{1,0:T(2,128)S(1)}, s32[2,64]{1,0:T(2,128)}, u32[]{:S(2)}) copy-start(s32[2,64]{1,0:T(2,128)} %param.27) | copy-start | bytes 1540
  7.2 156.2 %all-gather.17.cloned.1.call-start = ((), (), s32[]{:S(2)}) async-start(), calls=%async_computation.11 | async-start | bytes 1081344 | tf_op jit(solution)/shard_map/all_gather | solution.py:49
  7.9 329.4 %reduce-scatter.12.cloned.1.call-start = ((), (), s32[]{:S(2)}) async-start(), calls=%async_computation.5 | async-start | bytes 2162688 | tf_op jit(solution)/shard_map/reduce_scatter | solution.py:53
  104.7 58.7 %copy-start.7 = (f32[1,2,64,2048]{3,2,1,0:T(8,128)S(1)}, f32[1,2,64,2048]{3,2,1,0:T(8,128)}, u32[]{:S(2)}) copy-start(f32[1,2,64,2048]{3,2,1,0:T(8,128)} %param.21) | copy-start | bytes 3145732
  163.3 4.3 copy-start.4
  172.1 1.6 copy-start.12
  173.6 401.4 %reduce-scatter.16.cloned.1.call-start = ((), (), s32[]{:S(2)}) async-start(), calls=%async_computation.12 | async-start | bytes 1081344
  338.2 70.6 %collective-permute-start = (f32[128,128]{0,1:T(8,128)S(1)}, f32[128,128]{0,1:T(8,128)S(1)}, u32[]{:S(2)}, u32[]{:S(2)}) collective-permute-start(f32[128,128]{0,1:T(8,128)S(1)} %sub.65), channel_id=1, source_target_pairs={{0,32},{32,0},{64,96},{96,64},{1,33},{33,1},{65,97},{97,65},{2,34}... | collective-permute-start | bytes 196616 | tf_op jit(solution)/shard_map/ppermute | solution.py:10
  417.1 336.0 %reduce-scatter.14.cloned.1.call-start = ((), (), s32[]{:S(2)}) async-start(), calls=%async_computation.6 | async-start | bytes 4325376 | tf_op jit(solution)/shard_map/reduce_scatter | solution.py:53
  575.0 6.1 copy-start.2
  575.0 6.1 copy-start.10
  588.3 346.2 %reduce-scatter.18.cloned.1.call-start = ((), (), s32[]{:S(2)}) async-start(), calls=%async_computation.13 | async-start | bytes 1081344 | tf_op jit(solution)/shard_map/reduce_scatter | solution.py:53
  778.0 306.0 %all-gather.9.cloned.1.call-start = ((), (), s32[]{:S(2)}) async-start(), calls=%async_computation.7 | async-start | bytes 1081344 | tf_op jit(solution)/shard_map/all_gather | solution.py:49
  934.6 327.7 %all-gather.11.cloned.1.call-start = ((), (), s32[]{:S(2)}) async-start(), calls=%async_computation.8 | async-start | bytes 4325376 | tf_op jit(solution)/shard_map/all_gather | solution.py:49
  1104.5 326.9 %all-gather.13.cloned.1.call-start = ((), (), s32[]{:S(2)}) async-start(), calls=%async_computation.9 | async-start | bytes 1081344 | tf_op jit(solution)/shard_map/all_gather | solution.py:49
  1262.3 10.3 copy-start.3
  1262.3 10.4 copy-start.5
  1280.6 285.2 %all-gather.15.cloned.1.call-start = ((), (), s32[]{:S(2)}) async-start(), calls=%async_computation.10 | async-start | bytes 2162688 | tf_op jit(solution)/shard_map/all_gather | solution.py:49
  1438.2 1.3 collective-permute-start.1
  1440.2 299.7 %reduce-scatter.20.cloned.1.call-start = ((), (), s32[]{:S(2)}) async-start(), calls=%async_computation.14 | async-start | bytes 1081344
  1565.8 5.8 copy-start.6
  1576.4 165.1 %copy-start.1 = (s32[2,64]{1,0:T(2,128)S(1)}, s32[2,64]{1,0:T(2,128)}, u32[]{:S(2)}) copy-start(s32[2,64]{1,0:T(2,128)} %param.27) | copy-start | bytes 1540
  1577.5 1.6 copy-start.8
  1577.5 2.4 copy-start.9
  (1 other events, 0.9 us)
Sparse Core Ops, SparseCore 0:
  9.7 153.6 all-gather.16
  173.8 163.5 reduce-scatter.11
  417.2 157.7 reduce-scatter.15
  588.5 164.5 reduce-scatter.13
  778.1 156.4 reduce-scatter.17
  936.2 147.7 all-gather.8
  1104.6 157.6 all-gather.10
  1280.7 150.7 all-gather.12
  1440.3 125.4 all-gather.14
  1579.2 160.5 reduce-scatter.19
